TPU v7x, 32 devices: a whole 2x2x4 slice. The times are simulated.
32 devices in a mesh: seq: 8 (over y, x, core), head: 4 (over z).
Axes of the slice: x: 2, y: 2, z: 4, core: 2. Of those that a mesh axis runs over, the one named last changes fastest.
Arguments:
- query: bfloat16 [2048, 4096], P('seq', 'head'), may hold values from -6 to 6
- key: bfloat16 [2048, 4096], P('seq', 'head'), may hold values from -6 to 6
- value: bfloat16 [2048, 4096], P('seq', 'head'), may hold values from -6 to 6
- head_gain: float32 [4096], P('head'), may hold values from 0.1 to 1.9
- out_weight: bfloat16 [4096, 4096], P('head', 'seq'), may hold values from -0.09375 to 0.09375
- stream: bfloat16 [2048, 4096], P(('seq', 'head')), may hold values from -6 to 6
- model_gain: float32 [4096], replicated, may hold values from 0.1 to 1.9
- expert_ids: int32 [2048, 8], P(('seq', 'head')), may hold values from 0 to 31, all different within a row; in each aligned block of 64 rows (0 to 63, 64 to 127, ...) at most 24 rows name the same one
- expert_gates: float32 [2048, 8], P(('seq', 'head')), may hold values from 0.1 to 0.5
- gate_weight: bfloat16 [32, 4096, 768], P(('seq', 'head')), may hold values from -0.09375 to 0.09375
- up_weight: bfloat16 [32, 4096, 768], P(('seq', 'head')), may hold values from -0.09375 to 0.09375
- down_weight: bfloat16 [32, 768, 4096], P(('seq', 'head')), may hold values from -0.21875 to 0.21875
- weight_scales: float32 [32, 3], P(('seq', 'head')), may hold values from 0.6 to 1.6
Outputs:
- layer_out: bfloat16 [2048, 4096], P(('seq', 'head'))
Inputs may be any that keep to these rules, and one draw needn't show every extreme that they name: `expert_ids`: among the 64 tokens of one device (aligned blocks of rows), no expert is named more than 24 times, a bound that some block reaches; the entries of one row differ.
All inputs are finite; a program needn't handle non-finite values.
Results may differ from a plain program's by a relative error of at most 0.013.
Values may be sent and summed in bfloat16 or wider, within the bound.
A program may use at most 128 MiB of HBM per device.

v0:
```python
import functools

import jax
import jax.numpy as jnp
from jax import lax
from jax.experimental import pallas as pl
from jax.experimental.pallas import tpu as pltpu
from jax.sharding import PartitionSpec as P

HD = 128
SEG = 128
TOPK = 8
MESH = pl.DeviceIdType.MESH


def layer_kernel(
    seqs,
    heads,
    slots,
    q_hbm,
    k_hbm,
    v_hbm,
    gain_ref,
    w_hbm,
    stream_hbm,
    model_ref,
    ids_ref,
    gates_ref,
    scale_ref,
    gate_hbm,
    up_hbm,
    down_hbm,
    out_ref,
    q_ref,
    k_ref,
    v_ref,
    stream_ref,
    state,
    mixed,
    normed_heads,
    wbuf,
    tot,
    own,
    psend,
    precv,
    res,
    square,
    route_ids,
    route_gates,
    pick_ref,
    mix_ref,
    gate_v,
    up_v,
    gath,
    send,
    recv,
    back,
    rgath,
    rsend,
    rrecv,
    acc_g,
    acc_u,
    act,
    sds,
    sdr,
    sfs,
    sfr,
    wds,
    wdr,
    wfs,
    wfr,
    ids_s,
    ids_r,
    gts_s,
    gts_r,
    zs,
    zr,
    gs,
    gr,
    ps,
    pr,
    rs,
    rr,
    cs,
    cr,
    load_sem,
    wown_sem,
    wsem,
    dsem,
    osem,
    bsem,
):
    s = lax.axis_index("seq")
    h = lax.axis_index("head")
    tokens, features = q_ref.shape
    rows, width = stream_ref.shape
    hidden = gate_v.shape[1]
    local = features // HD
    block = w_hbm.shape[1]
    subs = block // SEG
    owners = seqs // 2
    chunks = 2 * subs
    step = owners * SEG
    halves = 2
    part = features // halves
    bits = [2**i for i in range(1, seqs.bit_length() - 1)]
    orders = [bits, bits[::-1]]
    evens = list(range(0, seqs, 2))
    far = sorted(range(1, seqs), key=lambda d: (-(d // 2).bit_count(), d))
    f32, bf = jnp.float32, jnp.bfloat16

    def flip(d):
        out, bit = s, 1
        while bit < seqs:
            if d & bit:
                out = out + bit * (1 - 2 * ((s // bit) % 2))
            bit *= 2
        return out

    partner = flip(1)

    def line(d):
        return lax.rem(h + d, heads)

    def cols(c):
        return pl.ds(pl.multiple_of(c * step, step), step)

    def seg(c, i):
        return pl.ds(pl.multiple_of(c * step + i * SEG, SEG), SEG)

    def home(c, i):
        at = (2 * i + c % 2) * block + (c // 2) * SEG
        return pl.ds(pl.multiple_of(at, SEG), SEG)

    def remote(src, dst, ssem, rsem, seq, head):
        return pltpu.make_async_remote_copy(
            src_ref=src,
            dst_ref=dst,
            send_sem=ssem,
            recv_sem=rsem,
            device_id=(seq, head),
            device_id_type=MESH,
        )

    def state_direct(slot, peer):
        return remote(state.at[slot], state.at[slot], sds.at[peer], sdr.at[slot], peer, h)

    def state_pass(slot):
        return remote(state.at[slot], state.at[slot], sfs.at[slot], sfr.at[slot], partner, h)

    def w_src(j, half):
        return w_hbm.at[pl.ds(half * part, part), pl.ds(pl.multiple_of(j * SEG, SEG), SEG)]

    def w_at(slot, j, half):
        return wbuf.at[
            2 * j + slot % 2,
            pl.ds(half * part, part),
            pl.ds(pl.multiple_of((slot // 2) * SEG, SEG), SEG),
        ]

    def w_first(j, half, bit):
        return remote(
            w_src(j, half), w_at(s, j, half),
            wds.at[s, j, half, bits.index(bit)], wdr.at[s, j, half], flip(bit), h,
        )

    def w_relay(slot, j, half, bit):
        return remote(
            w_at(slot, j, half), w_at(slot, j, half),
            wds.at[slot, j, half, bits.index(bit)], wdr.at[slot, j, half], flip(bit), h,
        )

    def later_bits(d, half):
        order = orders[half]
        last = max(order.index(bit) for bit in bits if d & bit)
        return order[last + 1 :]

    def w_pass(slot, j, half):
        return remote(
            w_at(slot, j, half), w_at(slot, j, half),
            wfs.at[slot, j, half], wfr.at[slot, j, half], partner, h,
        )

    def w_own_pass(j, half):
        return remote(
            w_src(j, half), w_at(s, j, half), wfs.at[s, j, half], wfr.at[s, j, half], partner, h
        )

    def w_own(j, half):
        return pltpu.make_async_copy(w_src(j, half), w_at(s, j, half), wown_sem.at[j, half])

    def w_start(j):
        for i in range(len(bits)):
            for half in range(halves):
                w_first(j, half, orders[half][i]).start()
        for half in range(halves):
            w_own_pass(j, half).start()

    def w_near(j):
        for half in range(halves):
            for d in evens:
                if d.bit_count() == 1:
                    w_relay(flip(d), j, half, bits[0]).wait_recv()
                    for bit in later_bits(d, half):
                        w_relay(flip(d), j, half, bit).start()
                    w_pass(flip(d), j, half).start()

    def w_far(j):
        for half in range(halves):
            for d in sorted(evens, key=lambda d: (d.bit_count(), d)):
                if d.bit_count() > 1:
                    w_relay(flip(d), j, half, bits[0]).wait_recv()
                    for bit in later_bits(d, half):
                        w_relay(flip(d), j, half, bit).start()
                    w_pass(flip(d), j, half).start()

    def w_passed(j):
        for half in range(halves):
            w_own(j, half).wait()
            for d in evens:
                w_pass(flip(d + 1), j, half).wait_recv()

    def w_drain(j):
        for half in range(halves):
            for bit in bits:
                w_first(j, half, bit).wait_send()
            w_own_pass(j, half).wait_send()
            for d in evens[1:]:
                for bit in later_bits(d, half):
                    w_relay(flip(d), j, half, bit).wait_send()
                w_pass(flip(d), j, half).wait_send()

    def ids_copy(slot, target):
        return remote(ids_ref, route_ids.at[slot], ids_s.at[target], ids_r.at[slot], s, target)

    def gates_copy(slot, target):
        return remote(
            gates_ref, route_gates.at[slot], gts_s.at[target], gts_r.at[slot], s, target
        )

    def weights(c, i):
        return (
            pltpu.make_async_copy(
                gate_hbm.at[0, home(c, i), :], gate_v.at[seg(c, i), :], wsem.at[0, c, i]
            ),
            pltpu.make_async_copy(
                up_hbm.at[0, home(c, i), :], up_v.at[seg(c, i), :], wsem.at[1, c, i]
            ),
        )

    def down_copy(c):
        return pltpu.make_async_copy(
            down_hbm.at[0, :, cols(c)], wbuf.at[c, pl.ds(0, hidden), :], dsem.at[c]
        )

    barrier = pltpu.get_barrier_semaphore()
    for d in range(1, seqs):
        pl.semaphore_signal(barrier, inc=1, device_id=(flip(d), h), device_id_type=MESH)
    for d in range(1, heads):
        pl.semaphore_signal(barrier, inc=1, device_id=(s, line(d)), device_id_type=MESH)
    loads = [
        pltpu.make_async_copy(source, target, load_sem.at[i])
        for i, (source, target) in enumerate(
            [(k_hbm, k_ref), (v_hbm, v_ref), (q_hbm, q_ref), (stream_hbm, stream_ref)]
        )
    ]
    for load in loads:
        load.start()

    def own_weights(j, carry):
        for half in range(halves):
            w_own(j, half).start()
        return carry

    lax.fori_loop(0, subs, own_weights, 0)
    route_ids[h] = ids_ref[...]
    route_gates[h] = gates_ref[...]
    loads[0].wait()
    loads[1].wait()

    def lanes(i):
        return pl.ds(pl.multiple_of(i * HD, HD), HD)

    def block_state(i, carry):
        total = lax.dot_general(
            k_ref[:, lanes(i)], v_ref[:, lanes(i)], (((0,), (0,)), ((), ())),
            preferred_element_type=f32,
        )
        state[s, i] = total.astype(bf)
        return carry

    lax.fori_loop(0, local, block_state, 0)
    pl.semaphore_wait(barrier, seqs + heads - 2)
    for d in range(2, seqs, 2):
        state_direct(s, flip(d)).start()
    state_pass(s).start()
    for d in range(1, heads):
        ids_copy(h, line(d)).start()
        gates_copy(h, line(d)).start()
    for j in range(min(2, subs)):
        w_start(j)

    def start_weights(c, carry):
        for i in range(owners):
            for copy in weights(c, i):
                copy.start()
        return carry

    lax.fori_loop(0, chunks, start_weights, 0)
    loads[2].wait()

    row = lax.broadcasted_iota(jnp.int32, (tokens, tokens), 0)
    col = lax.broadcasted_iota(jnp.int32, (tokens, tokens), 1)
    causal = col <= row

    def local_part(i, carry):
        scores = lax.dot_general(
            q_ref[:, lanes(i)], k_ref[:, lanes(i)], (((1,), (1,)), ((), ())),
            preferred_element_type=f32,
        )
        scores = jnp.where(causal, scores, 0.0).astype(bf)
        mixed[:, lanes(i)] = jnp.dot(scores, v_ref[:, lanes(i)], preferred_element_type=f32)
        return carry

    lax.fori_loop(0, local, local_part, 0)

    for d in range(1, heads):
        ids_copy(line(d), line(d)).wait_recv()
        gates_copy(line(d), line(d)).wait_recv()
    ids = route_ids[...].reshape(tokens, TOPK)
    gates = route_gates[...].reshape(tokens, TOPK)
    lane = lax.broadcasted_iota(jnp.int32, (tokens, 128), 1)
    hits = jnp.zeros((tokens, 128), f32)
    shares = jnp.zeros((tokens, 128), f32)
    for n in range(seqs):
        chosen = ids == n * heads + h
        hit = jnp.sum(jnp.where(chosen, 1.0, 0.0), axis=1, keepdims=True)
        share = jnp.sum(jnp.where(chosen, gates, 0.0), axis=1, keepdims=True)
        hits = jnp.where(lane == n, hit, hits)
        shares = jnp.where(lane == n, share, shares)
    earlier = jnp.where(col < row, 1.0, 0.0).astype(bf)
    rank = jnp.dot(earlier, hits.astype(bf), preferred_element_type=f32)
    place = jnp.where(hits > 0.5, rank, -1.0)
    spread_row = lax.broadcasted_iota(jnp.int32, (128, seqs * slots), 0)
    spread_col = lax.broadcasted_iota(jnp.int32, (128, seqs * slots), 1)
    inside = (spread_col >= spread_row * slots) & (spread_col < spread_row * slots + slots)
    spread = jnp.where(inside, 1.0, 0.0).astype(bf)
    slot_at = lax.broadcasted_iota(jnp.int32, (tokens, seqs * slots), 1)
    base = jnp.zeros((tokens, seqs * slots), jnp.int32)
    for n in range(1, seqs):
        base = jnp.where(slot_at >= n * slots, n * slots, base)
    slot_at = (slot_at - base).astype(f32)
    taken = jnp.dot(place.astype(bf), spread, preferred_element_type=f32) == slot_at
    shared = jnp.dot(shares.astype(bf), spread, preferred_element_type=f32)
    mix_ref[...] = jnp.where(taken, shared, 0.0).astype(bf)
    pick_ref[...] = jnp.where(taken, 1.0, 0.0).T.astype(bf)

    for d in range(2, seqs, 2):
        state_direct(flip(d), flip(d)).wait_recv()
        state_pass(flip(d)).start()
    for d in range(1, seqs, 2):
        state_pass(flip(d)).wait_recv()

    def earlier_part(i, carry):
        prior = jnp.zeros((HD, HD), f32)
        for c in range(seqs):
            prior = prior + jnp.where(c < s, state[c, i].astype(f32), 0.0)
        total = mixed[:, lanes(i)] + jnp.dot(
            q_ref[:, lanes(i)], prior.astype(bf), preferred_element_type=f32
        )
        mean_square = jnp.mean(total * total, axis=-1, keepdims=True)
        normed_heads[:, lanes(i)] = (
            total * lax.rsqrt(mean_square + 1e-06) * gain_ref[:, lanes(i)]
        ).astype(bf)
        return carry

    lax.fori_loop(0, local, earlier_part, 0)

    def sum_copy(sems, c, d):
        return remote(
            psend.at[line(d), :, cols(c)], precv.at[h, :, cols(c)],
            sems[0].at[c, d], sems[1].at[c, h], s, line(d),
        )

    def sum_arrival(sems, c, source):
        return remote(
            psend.at[source, :, cols(c)], precv.at[source, :, cols(c)],
            sems[0].at[c, 0], sems[1].at[c, source], s, source,
        )

    def gather_copy(c, d, source, target):
        at = gath.at[source, :, cols(c)]
        return remote(at, at, gs.at[c, d], gr.at[c, source], s, target)

    def rgather_copy(d, source, target):
        at = rgath.at[source]
        return remote(at, at, gs.at[chunks, d], gr.at[chunks, source], s, target)

    def plane_copy(c, d):
        return remote(
            send.at[flip(d), :, cols(c)], recv.at[s, :, cols(c)], ps.at[c, d], pr.at[c, s],
            flip(d), h,
        )

    def plane_arrival(c, source):
        return remote(
            send.at[source, :, cols(c)], recv.at[source, :, cols(c)], ps.at[c, 0],
            pr.at[c, source], source, h,
        )

    def own_copy(c):
        return pltpu.make_async_copy(
            send.at[s, :, cols(c)], recv.at[s, :, cols(c)], osem.at[c]
        )

    def rplane_copy(d):
        return remote(
            rsend.at[flip(d)], rrecv.at[s], ps.at[chunks, d], pr.at[chunks, s], flip(d), h
        )

    def rplane_arrival(source):
        return remote(
            rsend.at[source], rrecv.at[source], ps.at[chunks, 0], pr.at[chunks, source],
            source, h,
        )

    def rown_copy():
        return pltpu.make_async_copy(rsend.at[s], rrecv.at[s], osem.at[chunks])

    def split_heads(total, c, sems):
        tot[...] = total.reshape(heads, rows, step)
        own[:, cols(c)] = tot[h]
        psend[:, :, cols(c)] = tot[...].astype(bf)
        for d in range(1, heads):
            sum_copy(sems, c, d).start()

    def project(c):
        total = jnp.dot(
            normed_heads[...], wbuf[c, pl.ds(0, features), :], preferred_element_type=f32
        )
        split_heads(total, c, (zs, zr))

    def settle(c):
        for d in range(1, heads):
            sum_arrival((zs, zr), c, line(d)).wait_recv()
        for i in range(owners):
            total = own[:, seg(c, i)]
            for d in range(1, heads):
                total = total + precv[line(d), :, seg(c, i)].astype(f32)
            residual = (stream_ref[:, home(c, i)].astype(f32) + total).astype(bf)
            res[:, home(c, i)] = residual
            value = residual.astype(f32)
            square[...] += value * value
            gath[h, :, seg(c, i)] = (value * model_ref[:, home(c, i)]).astype(bf)
        for d in range(1, heads):
            gather_copy(c, d, h, line(d)).start()

    def settle_norm():
        mean_square = jnp.sum(square[...], axis=1, keepdims=True) / width
        factor = jnp.broadcast_to(lax.rsqrt(mean_square + 1e-06), (rows, 128))
        high = factor.astype(bf).astype(f32)
        low = (factor - high).astype(bf).astype(f32)
        at = lax.broadcasted_iota(jnp.int32, (rows, 128), 1)
        rgath[h] = jnp.where(at < 64, high, low).astype(bf)
        for d in range(1, heads):
            rgather_copy(d, h, line(d)).start()

    def dispatch(c):
        for d in range(1, heads):
            gather_copy(c, d, line(d), line(d)).wait_recv()
        picked = jnp.dot(
            pick_ref[...], gath[:, :, cols(c)].reshape(tokens, step),
            preferred_element_type=f32,
        )
        send[:, :, cols(c)] = picked.astype(bf).reshape(seqs, slots, step)
        for d in far:
            plane_copy(c, d).start()
        own_copy(c).start()

    def dispatch_norm():
        for d in range(1, heads):
            rgather_copy(d, line(d), line(d)).wait_recv()
        picked = jnp.dot(
            pick_ref[...], rgath[...].reshape(tokens, 128), preferred_element_type=f32
        )
        rsend[...] = picked.astype(bf).reshape(seqs, slots, 128)
        for d in far:
            rplane_copy(d).start()
        rown_copy().start()

    def expand(c):
        for i in range(owners):
            for copy in weights(c, i):
                copy.wait()
        for d in range(1, seqs):
            plane_arrival(c, flip(d)).wait_recv()
        own_copy(c).wait()
        lhs = recv[:, :, cols(c)].reshape(seqs * slots, step)
        acc_g[...] += jnp.dot(lhs, gate_v[cols(c), :], preferred_element_type=f32)
        acc_u[...] += jnp.dot(lhs, up_v[cols(c), :], preferred_element_type=f32)

    acc_g[...] = jnp.zeros_like(acc_g)
    acc_u[...] = jnp.zeros_like(acc_u)
    square[...] = jnp.zeros_like(square)
    loads[3].wait()

    w_near(0)
    if subs > 2:
        w_start(2)
    if subs > 1:
        w_near(1)
    w_far(0)
    w_passed(0)
    depth = 4

    def forward(t, carry):
        @pl.when(t < chunks)
        def _():
            project(t)

        @pl.when((t >= 1) & (t <= chunks))
        def _():
            settle(t - 1)

        @pl.when(t == chunks)
        def _():
            settle_norm()

        @pl.when((t >= 2) & (t <= chunks + 1))
        def _():
            dispatch(t - 2)

        @pl.when(t == chunks + 1)
        def _():
            dispatch_norm()

        @pl.when(t >= depth)
        def _():
            expand(t - depth)

        @pl.when(t + 3 < subs)
        def _():
            w_start(t + 3)

        @pl.when(t + 2 < subs)
        def _():
            w_near(t + 2)

        @pl.when(t + 1 < subs)
        def _():
            w_far(t + 1)
            w_passed(t + 1)

        return carry

    lax.fori_loop(0, chunks + depth, forward, 0)

    def release(j, carry):
        w_drain(j)
        return carry

    def start_down(c, carry):
        down_copy(c).start()
        return carry

    lax.fori_loop(0, subs, release, 0)
    lax.fori_loop(0, chunks, start_down, 0)

    for d in range(1, seqs):
        rplane_arrival(flip(d)).wait_recv()
    rown_copy().wait()
    gate_scale = scale_ref[0, 0]
    up_scale = scale_ref[0, 1]
    down_scale = scale_ref[0, 2]

    def activate(i, carry):
        at = pl.ds(pl.multiple_of(i * slots, slots), slots)
        factor = jnp.sum(rrecv[i].astype(f32), axis=1, keepdims=True) / 64
        g = acc_g[at, :] * (factor * gate_scale)
        u = acc_u[at, :] * (factor * up_scale)
        act[at, :] = (g / (1.0 + jnp.exp(-g)) * u).astype(bf)
        return carry

    lax.fori_loop(0, seqs, activate, 0)

    def back_copy(c, d):
        return remote(
            recv.at[flip(d), :, cols(c)], back.at[s, :, cols(c)], rs.at[c, d], rr.at[c, s],
            flip(d), h,
        )

    def back_arrival(c, source):
        return remote(
            recv.at[source, :, cols(c)], back.at[source, :, cols(c)], rs.at[c, 0],
            rr.at[c, source], source, h,
        )

    def own_back(c):
        return pltpu.make_async_copy(
            recv.at[s, :, cols(c)], back.at[s, :, cols(c)], bsem.at[c]
        )

    def contract(c, carry):
        down_copy(c).wait()
        rows_out = jnp.dot(
            act[...], wbuf[c, pl.ds(0, hidden), :], preferred_element_type=f32
        )
        recv[:, :, cols(c)] = (rows_out * down_scale).astype(bf).reshape(seqs, slots, step)
        for d in far:
            back_copy(c, d).start()
        own_back(c).start()
        for d in range(1, heads):
            sum_copy((zs, zr), c, d).wait_send()
        return carry

    lax.fori_loop(0, chunks, contract, 0)

    def combine(c):
        for d in range(1, seqs):
            back_arrival(c, flip(d)).wait_recv()
        own_back(c).wait()
        total = jnp.dot(
            mix_ref[...], back[:, :, cols(c)].reshape(seqs * slots, step),
            preferred_element_type=f32,
        )
        split_heads(total, c, (cs, cr))

    def finish(c):
        total = res[:, cols(c)].astype(f32) + own[:, cols(c)]
        for d in range(1, heads):
            sum_arrival((cs, cr), c, line(d)).wait_recv()
            total = total + precv[line(d), :, cols(c)].astype(f32)
        out_ref[:, cols(c)] = total.astype(bf)

    def backward(t, carry):
        @pl.when(t < chunks)
        def _():
            combine(t)

        @pl.when(t >= 1)
        def _():
            finish(t - 1)

        return carry

    lax.fori_loop(0, chunks + 1, backward, 0)

    for d in range(2, seqs, 2):
        state_direct(s, flip(d)).wait_send()
    for d in evens:
        state_pass(flip(d)).wait_send()
    for d in range(1, heads):
        ids_copy(h, line(d)).wait_send()
        gates_copy(h, line(d)).wait_send()
        rgather_copy(d, h, line(d)).wait_send()
    for d in range(1, seqs):
        rplane_copy(d).wait_send()

    def drain(c, carry):
        for d in range(1, heads):
            gather_copy(c, d, h, line(d)).wait_send()
            sum_copy((cs, cr), c, d).wait_send()
        for d in range(1, seqs):
            plane_copy(c, d).wait_send()
            back_copy(c, d).wait_send()
        return carry

    lax.fori_loop(0, chunks, drain, 0)


def body(
    query,
    key,
    value,
    head_gain,
    out_weight,
    stream,
    model_gain,
    expert_ids,
    expert_gates,
    gate_weight,
    up_weight,
    down_weight,
    weight_scales,
):
    seqs, heads = lax.axis_size("seq"), lax.axis_size("head")
    tokens, features = query.shape
    rows, width = stream.shape
    hidden = gate_weight.shape[2]
    local = features // HD
    block = out_weight.shape[1]
    subs = block // SEG
    owners = seqs // 2
    chunks = 2 * subs
    step = owners * SEG
    capacity = 3 * rows * TOPK // (2 * seqs * heads)
    slots = -(-capacity * heads // 16) * 16
    nbits = seqs.bit_length() - 2
    vmem = pl.BlockSpec(memory_space=pltpu.VMEM)
    smem = pl.BlockSpec(memory_space=pltpu.SMEM)
    anywhere = pl.BlockSpec(memory_space=pl.ANY)
    bf, f32 = jnp.bfloat16, jnp.float32
    dma = pltpu.SemaphoreType.DMA
    return pl.pallas_call(
        functools.partial(layer_kernel, seqs, heads, slots),
        out_shape=jax.ShapeDtypeStruct((rows, width), bf),
        in_specs=[anywhere] * 3 + [vmem] + [anywhere] * 2 + [vmem] * 3 + [smem] + [anywhere] * 3,
        out_specs=vmem,
        scratch_shapes=[
            pltpu.VMEM((tokens, features), bf),
            pltpu.VMEM((tokens, features), bf),
            pltpu.VMEM((tokens, features), bf),
            pltpu.VMEM((rows, width), bf),
            pltpu.VMEM((seqs, local, HD, HD), bf),
            pltpu.VMEM((tokens, features), f32),
            pltpu.VMEM((tokens, features), bf),
            pltpu.VMEM((chunks, max(features, hidden), step), bf),
            pltpu.VMEM((heads, rows, step), f32),
            pltpu.VMEM((rows, width), f32),
            pltpu.VMEM((heads, rows, width), bf),
            pltpu.VMEM((heads, rows, width), bf),
            pltpu.VMEM((rows, width), bf),
            pltpu.VMEM((rows, SEG), f32),
            pltpu.VMEM((heads, rows, TOPK), jnp.int32),
            pltpu.VMEM((heads, rows, TOPK), f32),
            pltpu.VMEM((seqs * slots, tokens), bf),
            pltpu.VMEM((tokens, seqs * slots), bf),
            pltpu.VMEM((width, hidden), bf),
            pltpu.VMEM((width, hidden), bf),
            pltpu.VMEM((heads, rows, width), bf),
            pltpu.VMEM((seqs, slots, width), bf),
            pltpu.VMEM((seqs, slots, width), bf),
            pltpu.VMEM((seqs, slots, width), bf),
            pltpu.VMEM((heads, rows, 128), bf),
            pltpu.VMEM((seqs, slots, 128), bf),
            pltpu.VMEM((seqs, slots, 128), bf),
            pltpu.VMEM((seqs * slots, hidden), f32),
            pltpu.VMEM((seqs * slots, hidden), f32),
            pltpu.VMEM((seqs * slots, hidden), bf),
            dma((seqs,)),
            dma((seqs,)),
            dma((seqs,)),
            dma((seqs,)),
            dma((seqs, subs, 2, nbits)),
            dma((seqs, subs, 2)),
            dma((seqs, subs, 2)),
            dma((seqs, subs, 2)),
            dma((heads,)),
            dma((heads,)),
            dma((heads,)),
            dma((heads,)),
            dma((chunks, heads)),
            dma((chunks, heads)),
            dma((chunks + 1, heads)),
            dma((chunks + 1, heads)),
            dma((chunks + 1, seqs)),
            dma((chunks + 1, seqs)),
            dma((chunks, seqs)),
            dma((chunks, seqs)),
            dma((chunks, heads)),
            dma((chunks, heads)),
            dma((4,)),
            dma((subs, 2)),
            dma((2, chunks, owners)),
            dma((chunks,)),
            dma((chunks + 1,)),
            dma((chunks,)),
        ],
        compiler_params=pltpu.CompilerParams(
            collective_id=0, has_side_effects=True, vmem_limit_bytes=67043328
        ),
    )(
        query,
        key,
        value,
        head_gain.reshape(1, -1),
        out_weight,
        stream,
        model_gain.reshape(1, -1),
        expert_ids,
        expert_gates,
        weight_scales,
        gate_weight,
        up_weight,
        down_weight,
    )


def solution(mesh):
    return jax.shard_map(
        body,
        mesh=mesh,
        in_specs=(
            P("seq", "head"),
            P("seq", "head"),
            P("seq", "head"),
            P("head"),
            P("head", "seq"),
            P(("seq", "head"), None),
            P(),
            P(("seq", "head"), None),
            P(("seq", "head"), None),
            P(("seq", "head"), None, None),
            P(("seq", "head"), None, None),
            P(("seq", "head"), None, None),
            P(("seq", "head"), None),
        ),
        out_specs=P(("seq", "head"), None),
        check_vma=False,
    )
```

profile of v0, /device:TPU:0, one launch (start us, length us, event | category | flops | bytes accessed | tf_op | source)
XLA Modules:
  0.0 239.1 jit_solution(8312954969330241218)
XLA Ops:
  0.0 1.4 copy.14.ids_ref
  1.4 1.4 copy.15.gates_ref
  2.8 234.4 %shard_map.127 = bf16[64,4096]{1,0:T(8,128)(2,1)} custom-call(bf16[256,1024]{1,0:T(8,128)(2,1)} %q_hbm.1, bf16[256,1024]{1,0:T(8,128)(2,1)} %k_hbm.1, bf16[256,1024]{1,0:T(8,128)(2,1)} %v_hbm.1, f32[1,1024]{1,0:T(1,128)} %bitcast.3, bf16[1024,512]{1,0:T(8,128)(2,1)} %w_hbm.1, bf16[64,4096]{1,0:T(8,128)(2,1)} %stream_hbm.1, f32[1,4096]{1,0:T(1,128)} %bitcast.2, ...), custom_call_target="tpu_custom_call" | custom-call | tf_op jit(solution)/shard_map/pallas_call | solution.py:704
  237.2 1.9 copy.17
where the time goes:
time: 240 us; the launch traced here: 239 us
  Pallas kernels  234 us (98%)
  local copies, waits for them, and re-layouts  4.62 us (2%)
    pallas_call x1, Pallas kernels, body(): pl.pallas_call(functools.partial(layer_kernel, seqs, heads, slots), out_s...  234 us

commit v1 on v0

v1 whole, which is shorter than its diff:
```python
import functools

import jax
import jax.numpy as jnp
from jax import lax
from jax.experimental import pallas as pl
from jax.experimental.pallas import tpu as pltpu
from jax.sharding import PartitionSpec as P

HD = 128
SEG = 128
TOPK = 8
MESH = pl.DeviceIdType.MESH


def layer_kernel(
    seqs,
    heads,
    slots,
    q_hbm,
    k_hbm,
    v_hbm,
    gain_ref,
    w_hbm,
    stream_hbm,
    model_ref,
    ids_ref,
    gates_ref,
    scale_ref,
    gate_hbm,
    up_hbm,
    down_hbm,
    out_ref,
    q_ref,
    k_ref,
    v_ref,
    stream_ref,
    state,
    pair_state,
    mixed,
    normed_heads,
    wbuf,
    tot,
    own,
    psend,
    precv,
    res,
    square,
    turn,
    route,
    pick_ref,
    mix_ref,
    gate_v,
    up_v,
    gath,
    send,
    recv,
    back,
    rgath,
    rsend,
    rrecv,
    acc_g,
    acc_u,
    act,
    swap_sem,
    pair_s,
    pair_r,
    fold_sem,
    wls,
    wlr,
    wfs,
    wfr,
    route_sem,
    zs,
    zl,
    zr,
    gs,
    gr,
    ps,
    pr,
    rs,
    rr,
    cs,
    cr,
    load_sem,
    wown_sem,
    wsem,
    dsem,
):
    s = lax.axis_index("seq")
    h = lax.axis_index("head")
    tokens, features = q_ref.shape
    rows, width = stream_ref.shape
    hidden = gate_v.shape[1]
    local = features // HD
    block = w_hbm.shape[1]
    subs = block // SEG
    owners = seqs // 2
    chunks = 2 * subs
    step = owners * SEG
    fine = step // 2
    pieces = 2 * chunks
    halves = 2
    part = features // halves
    bits = [2**i for i in range(1, seqs.bit_length() - 1)]
    orders = [bits, bits[::-1]]
    evens = list(range(0, seqs, 2))
    far = sorted(range(1, seqs), key=lambda d: (-(d // 2).bit_count(), d))
    f32, bf = jnp.float32, jnp.bfloat16
    core = s % 2
    relayed = heads == 4
    inner = (h == 1) | (h == 2)
    low = h // 2
    near = jnp.where(inner, 3 * low, 1 + low)
    other = jnp.where(inner, 3 - h, 2 - low)
    beyond = 3 - near
    first = jnp.where(inner, 1 - low, low)

    def flip(d):
        out, bit = s, 1
        while bit < seqs:
            if d & bit:
                out = out + bit * (1 - 2 * ((s // bit) % 2))
            bit *= 2
        return out

    partner = flip(1)

    def line(d):
        return lax.rem(h + d, heads)

    def cols(c):
        return pl.ds(pl.multiple_of(c * step, step), step)

    def fcols(c):
        return pl.ds(pl.multiple_of(c * fine, fine), fine)

    def seg(c, i):
        return pl.ds(pl.multiple_of(c * step + i * SEG, SEG), SEG)

    def home(c, i):
        at = (2 * i + c % 2) * block + (c // 2) * SEG
        return pl.ds(pl.multiple_of(at, SEG), SEG)

    def settled(ref, sem):
        pltpu.make_async_copy(ref, ref, sem).wait()

    def remote(src, dst, ssem, rsem, seq, head):
        return pltpu.make_async_remote_copy(
            src_ref=src,
            dst_ref=dst,
            send_sem=ssem,
            recv_sem=rsem,
            device_id=(seq, head),
            device_id_type=MESH,
        )

    def share(slot, half):
        return pair_state.at[slot // 2, pl.ds(half * (local // 2), local // 2)]

    def pair_direct(peer):
        at = share(s, core)
        return remote(at, at, pair_s, pair_r.at[s // 2], peer, h)

    def pair_pass(slot):
        at = share(slot, core)
        return remote(at, at, fold_sem.at[0], fold_sem.at[1], partner, h)

    def state_swap():
        return remote(state.at[0], state.at[1], swap_sem.at[0], swap_sem.at[1], partner, h)

    def w_src(j, half):
        return w_hbm.at[pl.ds(half * part, part), pl.ds(pl.multiple_of(j * SEG, SEG), SEG)]

    def w_at(slot, j, half):
        return wbuf.at[
            2 * j + slot % 2,
            pl.ds(half * part, part),
            pl.ds(pl.multiple_of((slot // 2) * SEG, SEG), SEG),
        ]

    def w_send(slot, j, half, bit, source):
        return remote(
            source, w_at(slot, j, half), wls.at[j], wlr.at[slot // 2, j, half], flip(bit), h
        )

    def w_pass(slot, j, half, source):
        return remote(source, w_at(slot, j, half), wfs.at[j], wfr.at[j], partner, h)

    def w_own(j):
        return pltpu.make_async_copy(
            w_hbm.at[:, pl.ds(pl.multiple_of(j * SEG, SEG), SEG)],
            wbuf.at[
                2 * j + core,
                pl.ds(0, features),
                pl.ds(pl.multiple_of((s // 2) * SEG, SEG), SEG),
            ],
            wown_sem.at[j],
        )

    def later_bits(d, half):
        order = orders[half]
        last = max(order.index(bit) for bit in bits if d & bit)
        return order[last + 1 :]

    def w_start(j):
        for i in range(len(bits)):
            for half in range(halves):
                w_send(s, j, half, orders[half][i], w_src(j, half)).start()
        for half in range(halves):
            w_pass(s, j, half, w_src(j, half)).start()

    def w_forward(d, j, half):
        slot = flip(d)
        at = w_at(slot, j, half)
        settled(at, wlr.at[slot // 2, j, half])
        for bit in later_bits(d, half):
            w_send(slot, j, half, bit, at).start()
        w_pass(slot, j, half, at).start()

    def w_near(j):
        for d in evens:
            if d.bit_count() == 1:
                for half in range(halves):
                    w_forward(d, j, half)

    def w_far(j):
        for d in sorted(evens, key=lambda d: (d.bit_count(), d)):
            if d.bit_count() > 1:
                for half in range(halves):
                    w_forward(d, j, half)

    def w_passed(j):
        w_own(j).wait()
        settled(wbuf.at[2 * j + 1 - core, pl.ds(0, features), :], wfr.at[j])

    def w_drain(j):
        settled(
            wbuf.at[2 * j, pl.ds(0, features), pl.ds(0, (owners - 1) * SEG)], wls.at[j]
        )
        settled(wbuf.at[2 * j, pl.ds(0, features), :], wfs.at[j])

    def route_copy(target):
        return remote(route.at[h], route.at[h], route_sem.at[0], route_sem.at[1], s, target)

    def weights(c, i):
        return (
            pltpu.make_async_copy(
                gate_hbm.at[0, home(c, i), :], gate_v.at[seg(c, i), :], wsem.at[0, c]
            ),
            pltpu.make_async_copy(
                up_hbm.at[0, home(c, i), :], up_v.at[seg(c, i), :], wsem.at[1, c]
            ),
        )

    def down_copy(c):
        return pltpu.make_async_copy(
            down_hbm.at[0, :, cols(c)], wbuf.at[c, pl.ds(0, hidden), :], dsem.at[c]
        )

    barrier = pltpu.get_barrier_semaphore()
    for d in range(1, seqs):
        pl.semaphore_signal(barrier, inc=1, device_id=(flip(d), h), device_id_type=MESH)
    for d in range(1, heads):
        pl.semaphore_signal(barrier, inc=1, device_id=(s, line(d)), device_id_type=MESH)
    loads = [
        pltpu.make_async_copy(source, target, load_sem.at[i])
        for i, (source, target) in enumerate(
            [(k_hbm, k_ref), (v_hbm, v_ref), (q_hbm, q_ref), (stream_hbm, stream_ref)]
        )
    ]
    for load in loads:
        load.start()
    pl.semaphore_wait(barrier, seqs + heads - 2)
    w_start(0)
    for n, source in enumerate((ids_ref[...].astype(f32), gates_ref[...])):
        turn[...] = jnp.zeros_like(turn)
        turn[pl.ds(0, TOPK), pl.ds(0, rows)] = source
        route[h, n] = turn[...].T[:rows, :]
    loads[0].wait()
    loads[1].wait()

    def lanes(i):
        return pl.ds(pl.multiple_of(i * HD, HD), HD)

    def block_state(i, carry):
        total = lax.dot_general(
            k_ref[:, lanes(i)], v_ref[:, lanes(i)], (((0,), (0,)), ((), ())),
            preferred_element_type=f32,
        )
        state[0, i] = total.astype(bf)
        return carry

    lax.fori_loop(0, local, block_state, 0)
    state_swap().start()
    for d in range(1, heads):
        route_copy(line(d)).start()

    def own_weights(j, carry):
        w_own(j).start()
        return carry

    lax.fori_loop(0, subs, own_weights, 0)
    state_swap().wait_recv()

    def pair_sum(i, carry):
        pair_state[s // 2, i] = (state[0, i].astype(f32) + state[1, i].astype(f32)).astype(bf)
        return carry

    lax.fori_loop(0, local, pair_sum, 0)
    for d in sorted(evens[1:], key=lambda d: (-d.bit_count(), d)):
        pair_direct(flip(d)).start()

    def start_weights(c, carry):
        for i in range(owners):
            for copy in weights(c, i):
                copy.start()
        return carry

    lax.fori_loop(0, chunks, start_weights, 0)
    loads[2].wait()

    row = lax.broadcasted_iota(jnp.int32, (tokens, tokens), 0)
    col = lax.broadcasted_iota(jnp.int32, (tokens, tokens), 1)
    causal = col <= row

    def local_part(i, carry):
        scores = lax.dot_general(
            q_ref[:, lanes(i)], k_ref[:, lanes(i)], (((1,), (1,)), ((), ())),
            preferred_element_type=f32,
        )
        scores = jnp.where(causal, scores, 0.0).astype(bf)
        mixed[:, lanes(i)] = jnp.dot(scores, v_ref[:, lanes(i)], preferred_element_type=f32)
        return carry

    lax.fori_loop(0, local, local_part, 0)

    w_near(0)
    if subs > 1:
        w_start(1)
    settled(route.at[pl.ds(0, heads - 1)], route_sem.at[1])

    def routing():
        ids = route[:, 0].reshape(tokens, 128)
        gates = route[:, 1].reshape(tokens, 128)
        lane = lax.broadcasted_iota(jnp.int32, (tokens, 128), 1)
        hits = jnp.zeros((tokens, 128), f32)
        shares = jnp.zeros((tokens, 128), f32)
        for n in range(seqs):
            chosen = (ids == (n * heads + h).astype(f32)) & (lane < TOPK)
            hit = jnp.sum(jnp.where(chosen, 1.0, 0.0), axis=1, keepdims=True)
            share = jnp.sum(jnp.where(chosen, gates, 0.0), axis=1, keepdims=True)
            hits = jnp.where(lane == n, hit, hits)
            shares = jnp.where(lane == n, share, shares)
        earlier = jnp.where(col < row, 1.0, 0.0).astype(bf)
        rank = jnp.dot(earlier, hits.astype(bf), preferred_element_type=f32)
        place = jnp.where(hits > 0.5, rank, -1.0)
        spread_row = lax.broadcasted_iota(jnp.int32, (128, seqs * slots), 0)
        spread_col = lax.broadcasted_iota(jnp.int32, (128, seqs * slots), 1)
        inside = (spread_col >= spread_row * slots) & (spread_col < spread_row * slots + slots)
        spread = jnp.where(inside, 1.0, 0.0).astype(bf)
        slot_at = lax.broadcasted_iota(jnp.int32, (tokens, seqs * slots), 1)
        base = jnp.zeros((tokens, seqs * slots), jnp.int32)
        for n in range(1, seqs):
            base = jnp.where(slot_at >= n * slots, n * slots, base)
        slot_at = (slot_at - base).astype(f32)
        taken = jnp.dot(place.astype(bf), spread, preferred_element_type=f32) == slot_at
        shared = jnp.dot(shares.astype(bf), spread, preferred_element_type=f32)
        mix_ref[...] = jnp.where(taken, shared, 0.0).astype(bf)
        pick_ref[...] = jnp.where(taken, 1.0, 0.0).T.astype(bf)

    routing()

    for d in evens[1:]:
        settled(share(flip(d), core), pair_r.at[flip(d) // 2])
        pair_pass(flip(d)).start()
    settled(pair_state.at[pl.ds(0, owners - 1), pl.ds(0, local // 2)], fold_sem.at[1])

    def earlier_part(i, carry):
        prior = jnp.where(core == 1, state[1, i].astype(f32), 0.0)
        for c in range(owners):
            prior = prior + jnp.where(c < s // 2, pair_state[c, i].astype(f32), 0.0)
        total = mixed[:, lanes(i)] + jnp.dot(
            q_ref[:, lanes(i)], prior.astype(bf), preferred_element_type=f32
        )
        mean_square = jnp.mean(total * total, axis=-1, keepdims=True)
        normed_heads[:, lanes(i)] = (
            total * lax.rsqrt(mean_square + 1e-06) * gain_ref[:, lanes(i)]
        ).astype(bf)
        return carry

    lax.fori_loop(0, local, earlier_part, 0)

    def split_heads(total, at, size):
        tot[:, :, pl.ds(0, size)] = total.reshape(heads, rows, size)
        own[:, at] = tot[h, :, pl.ds(0, size)]
        psend[:, :, at] = tot[:, :, pl.ds(0, size)].astype(bf)

    def sum_send(src, dst, sem, target):
        return remote(src, dst, zs, sem, s, target)

    def project(c):
        total = jnp.dot(
            normed_heads[...], wbuf[c, pl.ds(0, features), :], preferred_element_type=f32
        )
        at = cols(c)
        split_heads(total, at, step)
        if not relayed:
            for d in range(1, heads):
                sum_send(
                    psend.at[line(d), :, at], precv.at[h, :, at], zr.at[c], line(d)
                ).start()
            return

        @pl.when(inner)
        def _():
            sum_send(psend.at[near, :, at], precv.at[0, :, at], zr.at[c], near).start()

        @pl.when(jnp.logical_not(inner))
        def _():
            sum_send(
                psend.at[pl.ds(1 - low, 3), :, at], precv.at[pl.ds(0, 3), :, at], zl.at[c], near
            ).start()

    def merge(c):
        if not relayed:
            return
        at = cols(c)

        @pl.when(inner)
        def _():
            settled(precv.at[pl.ds(0, 3), :, at], zl.at[c])
            for target, slot in ((other, 3), (beyond, 1)):
                merged = psend[target, :, at].astype(f32) + precv[
                    target - first, :, at
                ].astype(f32)
                psend[target, :, at] = merged.astype(bf)
                sum_send(
                    psend.at[target, :, at], precv.at[slot, :, at], zr.at[c], target
                ).start()

    def gather_send(src, c, target):
        return remote(src, src, gs.at[0], gr.at[c], s, target)

    def settle(c):
        if relayed:

            @pl.when(inner)
            def _():
                settled(precv.at[3, :, cols(c)], zr.at[c])

            @pl.when(jnp.logical_not(inner))
            def _():
                settled(precv.at[pl.ds(0, 2), :, cols(c)], zr.at[c])

            sources = [jnp.where(inner, h - first, 0), jnp.where(inner, 3, 1)]
        else:
            settled(precv.at[pl.ds(0, heads - 1), :, cols(c)], zr.at[c])
            sources = [line(d) for d in range(1, heads)]
        for i in range(owners):
            total = own[:, seg(c, i)]
            for source in sources:
                total = total + precv[source, :, seg(c, i)].astype(f32)
            residual = (stream_ref[:, home(c, i)].astype(f32) + total).astype(bf)
            res[:, home(c, i)] = residual
            value = residual.astype(f32)
            square[...] += value * value
            gath[h, :, seg(c, i)] = (value * model_ref[:, home(c, i)]).astype(bf)
        for target in (near, other) if relayed else [line(d) for d in range(1, heads)]:
            gather_send(gath.at[h, :, cols(c)], c, target).start()

    def pass_on(c):
        if not relayed:
            return

        @pl.when(inner)
        def _():
            settled(gath.at[pl.ds(0, 3), :, cols(c)], gr.at[c])
            gather_send(gath.at[pl.ds(2 - 2 * low, 2), :, cols(c)], c, near).start()

    def settle_norm():
        mean_square = jnp.sum(square[...], axis=1, keepdims=True) / width
        factor = jnp.broadcast_to(lax.rsqrt(mean_square + 1e-06), (rows, 128))
        high = factor.astype(bf).astype(f32)
        rest = (factor - high).astype(bf).astype(f32)
        at = lax.broadcasted_iota(jnp.int32, (rows, 128), 1)
        rgath[h] = jnp.where(at < 64, high, rest).astype(bf)
        for d in range(1, heads):
            at = rgath.at[h]
            remote(at, at, gs.at[1], gr.at[chunks], s, line(d)).start()

    def own_copy(c):
        return pltpu.make_async_copy(send.at[s, :, cols(c)], recv.at[s, :, cols(c)], pr.at[c])

    def dispatch(c):
        def arrived():
            settled(gath.at[pl.ds(0, heads - 1), :, cols(c)], gr.at[c])

        if relayed:
            pl.when(jnp.logical_not(inner))(arrived)
        else:
            arrived()
        picked = jnp.dot(
            pick_ref[...], gath[:, :, cols(c)].reshape(tokens, step),
            preferred_element_type=f32,
        )
        send[:, :, cols(c)] = picked.astype(bf).reshape(seqs, slots, step)
        for d in far:
            remote(
                send.at[flip(d), :, cols(c)], recv.at[s, :, cols(c)], ps.at[0], pr.at[c],
                flip(d), h,
            ).start()
        own_copy(c).start()

    def dispatch_norm():
        settled(rgath.at[pl.ds(0, heads - 1)], gr.at[chunks])
        picked = jnp.dot(
            pick_ref[...], rgath[...].reshape(tokens, 128), preferred_element_type=f32
        )
        rsend[...] = picked.astype(bf).reshape(seqs, slots, 128)
        for d in far:
            remote(
                rsend.at[flip(d)], rrecv.at[s], ps.at[1], pr.at[chunks], flip(d), h
            ).start()
        pltpu.make_async_copy(rsend.at[s], rrecv.at[s], pr.at[chunks]).start()

    def expand(c):
        pltpu.make_async_copy(
            gate_hbm.at[0, pl.ds(0, step), :], gate_v.at[cols(c), :], wsem.at[0, c]
        ).wait()
        pltpu.make_async_copy(
            up_hbm.at[0, pl.ds(0, step), :], up_v.at[cols(c), :], wsem.at[1, c]
        ).wait()
        settled(recv.at[:, :, cols(c)], pr.at[c])
        lhs = recv[:, :, cols(c)].reshape(seqs * slots, step)
        acc_g[...] += jnp.dot(lhs, gate_v[cols(c), :], preferred_element_type=f32)
        acc_u[...] += jnp.dot(lhs, up_v[cols(c), :], preferred_element_type=f32)

    acc_g[...] = jnp.zeros_like(acc_g)
    acc_u[...] = jnp.zeros_like(acc_u)
    square[...] = jnp.zeros_like(square)
    loads[3].wait()

    w_far(0)
    w_passed(0)
    depth = 6

    def stage(t, lag, work):
        @pl.when((t >= lag) & (t < chunks + lag))
        def _():
            work(t - lag)

    def forward(t, carry):
        j = (t + 2) // 2

        @pl.when((t % 2 == 0) & (j < subs))
        def _():
            w_near(j)

        @pl.when((t % 2 == 0) & (j + 1 < subs))
        def _():
            w_start(j + 1)

        @pl.when((t % 2 == 1) & (j < subs))
        def _():
            w_far(j)
            w_passed(j)

        stage(t, 4, dispatch)
        stage(t, 3, pass_on)
        stage(t, 2, settle)

        @pl.when(t == chunks + 1)
        def _():
            settle_norm()

        stage(t, 1, merge)
        stage(t, 0, project)

        @pl.when(t == chunks + 3)
        def _():
            dispatch_norm()

        stage(t, depth, expand)
        return carry

    lax.fori_loop(0, chunks + depth, forward, 0)

    def release(j, carry):
        w_drain(j)
        return carry

    def start_down(c, carry):
        down_copy(c).start()
        return carry

    lax.fori_loop(0, subs, release, 0)
    lax.fori_loop(0, chunks, start_down, 0)
    settled(psend.at[pl.ds(0, heads - 1)], zs)
    settled(rrecv, pr.at[chunks])
    gate_scale = scale_ref[0, 0]
    up_scale = scale_ref[0, 1]
    down_scale = scale_ref[0, 2]

    def activate(i, carry):
        at = pl.ds(pl.multiple_of(i * slots, slots), slots)
        factor = jnp.sum(rrecv[i].astype(f32), axis=1, keepdims=True) / 64
        g = acc_g[at, :] * (factor * gate_scale)
        u = acc_u[at, :] * (factor * up_scale)
        act[at, :] = (g / (1.0 + jnp.exp(-g)) * u).astype(bf)
        return carry

    lax.fori_loop(0, seqs, activate, 0)

    def contract(c, carry):
        @pl.when(c % 2 == 0)
        def _():
            down_copy(c // 2).wait()

        at = fcols(c)
        rows_out = jnp.dot(
            act[...],
            wbuf[c // 2, pl.ds(0, hidden), pl.ds(pl.multiple_of((c % 2) * fine, fine), fine)],
            preferred_element_type=f32,
        )
        recv[:, :, at] = (rows_out * down_scale).astype(bf).reshape(seqs, slots, fine)
        for d in far:
            remote(
                recv.at[flip(d), :, at], back.at[s, :, at], rs, rr.at[c], flip(d), h
            ).start()
        pltpu.make_async_copy(recv.at[s, :, at], back.at[s, :, at], rr.at[c]).start()
        return carry

    lax.fori_loop(0, pieces, contract, 0)

    def combine(c):
        at = fcols(c)
        settled(back.at[:, :, at], rr.at[c])
        total = jnp.dot(
            mix_ref[...], back[:, :, at].reshape(seqs * slots, fine),
            preferred_element_type=f32,
        )
        split_heads(total, at, fine)
        for d in range(1, heads):
            remote(
                psend.at[line(d), :, at], precv.at[h, :, at], cs, cr.at[c], s, line(d)
            ).start()

    def finish(c):
        at = fcols(c)
        settled(precv.at[pl.ds(0, heads - 1), :, at], cr.at[c])
        total = res[:, at].astype(f32) + own[:, at]
        for d in range(1, heads):
            total = total + precv[line(d), :, at].astype(f32)
        out_ref[:, at] = total.astype(bf)

    def backward(t, carry):
        @pl.when(t < pieces)
        def _():
            combine(t)

        @pl.when(t >= 2)
        def _():
            finish(t - 2)

        return carry

    lax.fori_loop(0, pieces + 2, backward, 0)

    state_swap().wait_send()
    settled(pair_state.at[pl.ds(0, owners - 1), pl.ds(0, local // 2)], pair_s)
    settled(pair_state.at[pl.ds(0, owners - 1), pl.ds(0, local // 2)], fold_sem.at[0])
    settled(route.at[pl.ds(0, heads - 1)], route_sem.at[0])
    if relayed:

        @pl.when(inner)
        def _():
            settled(gath, gs.at[0])

        @pl.when(jnp.logical_not(inner))
        def _():
            settled(gath.at[pl.ds(0, 2)], gs.at[0])
    else:
        settled(gath.at[pl.ds(0, heads - 1)], gs.at[0])
    settled(rgath.at[pl.ds(0, heads - 1)], gs.at[1])
    settled(send.at[pl.ds(0, seqs - 1)], ps.at[0])
    settled(rsend.at[pl.ds(0, seqs - 1)], ps.at[1])
    settled(recv.at[pl.ds(0, seqs - 1)], rs)
    settled(psend.at[pl.ds(0, heads - 1)], cs)


def body(
    query,
    key,
    value,
    head_gain,
    out_weight,
    stream,
    model_gain,
    expert_ids,
    expert_gates,
    gate_weight,
    up_weight,
    down_weight,
    weight_scales,
):
    seqs, heads = lax.axis_size("seq"), lax.axis_size("head")
    tokens, features = query.shape
    rows, width = stream.shape
    hidden = gate_weight.shape[2]
    local = features // HD
    block = out_weight.shape[1]
    subs = block // SEG
    owners = seqs // 2
    chunks = 2 * subs
    step = owners * SEG
    capacity = 3 * rows * TOPK // (2 * seqs * heads)
    slots = -(-capacity * heads // 16) * 16
    vmem = pl.BlockSpec(memory_space=pltpu.VMEM)
    smem = pl.BlockSpec(memory_space=pltpu.SMEM)
    anywhere = pl.BlockSpec(memory_space=pl.ANY)
    bf, f32 = jnp.bfloat16, jnp.float32
    dma = pltpu.SemaphoreType.DMA
    return pl.pallas_call(
        functools.partial(layer_kernel, seqs, heads, slots),
        out_shape=jax.ShapeDtypeStruct((rows, width), bf),
        in_specs=[anywhere] * 3 + [vmem] + [anywhere] * 2 + [vmem] * 3 + [smem] + [anywhere] * 3,
        out_specs=vmem,
        scratch_shapes=[
            pltpu.VMEM((tokens, features), bf),
            pltpu.VMEM((tokens, features), bf),
            pltpu.VMEM((tokens, features), bf),
            pltpu.VMEM((rows, width), bf),
            pltpu.VMEM((2, local, HD, HD), bf),
            pltpu.VMEM((owners, local, HD, HD), bf),
            pltpu.VMEM((tokens, features), f32),
            pltpu.VMEM((tokens, features), bf),
            pltpu.VMEM((chunks, max(features, hidden), step), bf),
            pltpu.VMEM((heads, rows, step), f32),
            pltpu.VMEM((rows, width), f32),
            pltpu.VMEM((heads, rows, width), bf),
            pltpu.VMEM((heads, rows, width), bf),
            pltpu.VMEM((rows, width), bf),
            pltpu.VMEM((rows, SEG), f32),
            pltpu.VMEM((128, 128), f32),
            pltpu.VMEM((heads, 2, rows, 128), f32),
            pltpu.VMEM((seqs * slots, tokens), bf),
            pltpu.VMEM((tokens, seqs * slots), bf),
            pltpu.VMEM((width, hidden), bf),
            pltpu.VMEM((width, hidden), bf),
            pltpu.VMEM((heads, rows, width), bf),
            pltpu.VMEM((seqs, slots, width), bf),
            pltpu.VMEM((seqs, slots, width), bf),
            pltpu.VMEM((seqs, slots, width), bf),
            pltpu.VMEM((heads, rows, 128), bf),
            pltpu.VMEM((seqs, slots, 128), bf),
            pltpu.VMEM((seqs, slots, 128), bf),
            pltpu.VMEM((seqs * slots, hidden), f32),
            pltpu.VMEM((seqs * slots, hidden), f32),
            pltpu.VMEM((seqs * slots, hidden), bf),
            dma((2,)),
            dma,
            dma((owners,)),
            dma((2,)),
            dma((subs,)),
            dma((owners, subs, 2)),
            dma((subs,)),
            dma((subs,)),
            dma((2,)),
            dma,
            dma((chunks,)),
            dma((chunks,)),
            dma((2,)),
            dma((chunks + 1,)),
            dma((2,)),
            dma((chunks + 1,)),
            dma,
            dma((2 * chunks,)),
            dma,
            dma((2 * chunks,)),
            dma((4,)),
            dma((subs,)),
            dma((2, chunks)),
            dma((chunks,)),
        ],
        compiler_params=pltpu.CompilerParams(
            collective_id=0, has_side_effects=True, vmem_limit_bytes=67043328
        ),
    )(
        query,
        key,
        value,
        head_gain.reshape(1, -1),
        out_weight,
        stream,
        model_gain.reshape(1, -1),
        expert_ids.T,
        expert_gates.T,
        weight_scales,
        gate_weight,
        up_weight,
        down_weight,
    )


def solution(mesh):
    return jax.shard_map(
        body,
        mesh=mesh,
        in_specs=(
            P("seq", "head"),
            P("seq", "head"),
            P("seq", "head"),
            P("head"),
            P("head", "seq"),
            P(("seq", "head"), None),
            P(),
            P(("seq", "head"), None),
            P(("seq", "head"), None),
            P(("seq", "head"), None, None),
            P(("seq", "head"), None, None),
            P(("seq", "head"), None, None),
            P(("seq", "head"), None),
        ),
        out_specs=P(("seq", "head"), None),
        check_vma=False,
    )
```

time: 240 us -> 205 us (0.85)
  Pallas kernels: 234 us -> 203 us
  local copies, waits for them, and re-layouts: 4.62 us -> 1.87 us
    pallas_call x1, Pallas kernels: 234 us -> 203 us  [body(): pl.pallas_call(functools.partial(layer_kernel, seqs, heads, slots), out_s...]
    unnamed x3 -> x1, local copies, waits for them, and re-layouts: 4.62 us -> 1.87 us
where the time goes in v1:
time: 205 us
  Pallas kernels  203 us (99%)
    pallas_call x1, Pallas kernels, body(): pl.pallas_call(functools.partial(layer_kernel, seqs, heads, slots), out_s...  203 us

profile of v1, /device:TPU:0, one launch (start us, length us, event | category | flops | bytes accessed | tf_op | source)
XLA Modules:
  0.0 204.9 jit_solution(8566097902879012050)
XLA Ops:
  0.0 203.0 %shard_map.127 = bf16[64,4096]{1,0:T(8,128)(2,1)} custom-call(bf16[256,1024]{1,0:T(8,128)(2,1)} %q_hbm.1, bf16[256,1024]{1,0:T(8,128)(2,1)} %k_hbm.1, bf16[256,1024]{1,0:T(8,128)(2,1)} %v_hbm.1, f32[1,1024]{1,0:T(1,128)} %bitcast.5, bf16[1024,512]{1,0:T(8,128)(2,1)} %w_hbm.1, bf16[64,4096]{1,0:T(8,128)(2,1)} %stream_hbm.1, f32[1,4096]{1,0:T(1,128)} %bitcast.4, ...), custom_call_target="tpu_custom_call" | custom-call | tf_op jit(solution)/shard_map/pallas_call | solution.py:724
  203.0 1.9 copy.15

commit v2 on v1

--- a/solution.py
+++ b/solution.py
@@ -37,7 +37,6 @@
     stream_ref,
     state,
     pair_state,
-    mixed,
     normed_heads,
     wbuf,
     tot,
@@ -48,15 +47,19 @@
     square,
     turn,
     route,
+    near_route,
+    table,
     pick_ref,
     mix_ref,
     gate_v,
     up_v,
     gath,
+    nbr,
     send,
     recv,
     back,
     rgath,
+    rnbr,
     rsend,
     rrecv,
     acc_g,
@@ -71,15 +74,22 @@
     wfs,
     wfr,
     route_sem,
+    near_s,
+    near_r,
     zs,
     zl,
     zr,
     gs,
     gr,
+    ds,
+    nr,
     ps,
     pr,
     rs,
     rr,
+    rl,
+    es,
+    er,
     cs,
     cr,
     load_sem,
@@ -105,7 +115,11 @@
     bits = [2**i for i in range(1, seqs.bit_length() - 1)]
     orders = [bits, bits[::-1]]
     evens = list(range(0, seqs, 2))
-    far = sorted(range(1, seqs), key=lambda d: (-(d // 2).bit_count(), d))
+    woven = seqs == 8
+    ways = [(2, 4), (4, 2)] if woven else [(0, 0)]
+    lists = [[0, 1, b2, b2 + 1] for _, b2 in ways] if woven else [list(range(seqs))]
+    count = len(lists[0])
+    owned = count * slots
     f32, bf = jnp.float32, jnp.bfloat16
     core = s % 2
     relayed = heads == 4
@@ -142,6 +156,9 @@
         at = (2 * i + c % 2) * block + (c // 2) * SEG
         return pl.ds(pl.multiple_of(at, SEG), SEG)
 
+    def band(i, n=1):
+        return pl.ds(pl.multiple_of(i * rows, rows), n * rows)
+
     def settled(ref, sem):
         pltpu.make_async_copy(ref, ref, sem).wait()
 
@@ -273,15 +290,21 @@
         load.start()
     pl.semaphore_wait(barrier, seqs + heads - 2)
     w_start(0)
-    for n, source in enumerate((ids_ref[...].astype(f32), gates_ref[...])):
-        turn[...] = jnp.zeros_like(turn)
-        turn[pl.ds(0, TOPK), pl.ds(0, rows)] = source
-        route[h, n] = turn[...].T[:rows, :]
+    route[h] = jnp.zeros((2 * TOPK, 128), f32)
+    route[h, pl.ds(0, TOPK), pl.ds(0, rows)] = ids_ref[...].astype(f32)
+    route[h, pl.ds(TOPK, TOPK), pl.ds(0, rows)] = gates_ref[...]
     loads[0].wait()
     loads[1].wait()
 
     def lanes(i):
         return pl.ds(pl.multiple_of(i * HD, HD), HD)
+
+    def mixed(i):
+        across = hidden // HD
+        return (
+            pl.ds(pl.multiple_of((i // across) * tokens, tokens), tokens),
+            pl.ds(pl.multiple_of((i % across) * HD, HD), HD),
+        )
 
     def block_state(i, carry):
         total = lax.dot_general(
@@ -330,7 +353,7 @@
             preferred_element_type=f32,
         )
         scores = jnp.where(causal, scores, 0.0).astype(bf)
-        mixed[:, lanes(i)] = jnp.dot(scores, v_ref[:, lanes(i)], preferred_element_type=f32)
+        acc_g[mixed(i)] = jnp.dot(scores, v_ref[:, lanes(i)], preferred_element_type=f32)
         return carry
 
     lax.fori_loop(0, local, local_part, 0)
@@ -339,15 +362,28 @@
     if subs > 1:
         w_start(1)
     settled(route.at[pl.ds(0, heads - 1)], route_sem.at[1])
-
-    def routing():
-        ids = route[:, 0].reshape(tokens, 128)
-        gates = route[:, 1].reshape(tokens, 128)
+    if woven:
+        for o, (b1, _) in enumerate(ways):
+            remote(route, near_route.at[o], near_s, near_r.at[o], flip(b1), h).start()
+
+    def tables(o, who):
+        def turned(i, carry):
+            turn[...] = jnp.zeros_like(turn)
+            source = near_route.at[o, i] if who else route.at[i]
+            turn[pl.ds(0, TOPK), :] = source[pl.ds(0, TOPK), :]
+            turn[pl.ds(64, TOPK), :] = source[pl.ds(TOPK, TOPK), :]
+            table[i] = turn[...].T[:rows, :]
+            return carry
+
+        lax.fori_loop(0, heads, turned, 0)
+        ids = table[...].reshape(tokens, 128)
+        gates = pltpu.roll(ids, 64, 1)
         lane = lax.broadcasted_iota(jnp.int32, (tokens, 128), 1)
         hits = jnp.zeros((tokens, 128), f32)
         shares = jnp.zeros((tokens, 128), f32)
-        for n in range(seqs):
-            chosen = (ids == (n * heads + h).astype(f32)) & (lane < TOPK)
+        for n, d in enumerate(lists[o]):
+            expert = flip(d) * heads + h
+            chosen = (ids == expert.astype(f32)) & (lane < TOPK)
             hit = jnp.sum(jnp.where(chosen, 1.0, 0.0), axis=1, keepdims=True)
             share = jnp.sum(jnp.where(chosen, gates, 0.0), axis=1, keepdims=True)
             hits = jnp.where(lane == n, hit, hits)
@@ -355,21 +391,27 @@
         earlier = jnp.where(col < row, 1.0, 0.0).astype(bf)
         rank = jnp.dot(earlier, hits.astype(bf), preferred_element_type=f32)
         place = jnp.where(hits > 0.5, rank, -1.0)
-        spread_row = lax.broadcasted_iota(jnp.int32, (128, seqs * slots), 0)
-        spread_col = lax.broadcasted_iota(jnp.int32, (128, seqs * slots), 1)
+        spread_row = lax.broadcasted_iota(jnp.int32, (128, owned), 0)
+        spread_col = lax.broadcasted_iota(jnp.int32, (128, owned), 1)
         inside = (spread_col >= spread_row * slots) & (spread_col < spread_row * slots + slots)
         spread = jnp.where(inside, 1.0, 0.0).astype(bf)
-        slot_at = lax.broadcasted_iota(jnp.int32, (tokens, seqs * slots), 1)
-        base = jnp.zeros((tokens, seqs * slots), jnp.int32)
-        for n in range(1, seqs):
+        slot_at = lax.broadcasted_iota(jnp.int32, (tokens, owned), 1)
+        base = jnp.zeros((tokens, owned), jnp.int32)
+        for n in range(1, count):
             base = jnp.where(slot_at >= n * slots, n * slots, base)
         slot_at = (slot_at - base).astype(f32)
         taken = jnp.dot(place.astype(bf), spread, preferred_element_type=f32) == slot_at
         shared = jnp.dot(shares.astype(bf), spread, preferred_element_type=f32)
-        mix_ref[...] = jnp.where(taken, shared, 0.0).astype(bf)
-        pick_ref[...] = jnp.where(taken, 1.0, 0.0).T.astype(bf)
-
-    routing()
+        mix_ref[o, who] = jnp.where(taken, shared, 0.0).astype(bf)
+        pick_ref[o, who] = jnp.where(taken, 1.0, 0.0).T.astype(bf)
+
+    def routing():
+        if woven:
+            for o in range(2):
+                settled(near_route.at[o], near_r.at[o])
+        for o in range(len(ways)):
+            for who in range(2 if woven else 1):
+                tables(o, who)
 
     for d in evens[1:]:
         settled(share(flip(d), core), pair_r.at[flip(d) // 2])
@@ -380,7 +422,7 @@
         prior = jnp.where(core == 1, state[1, i].astype(f32), 0.0)
         for c in range(owners):
             prior = prior + jnp.where(c < s // 2, pair_state[c, i].astype(f32), 0.0)
-        total = mixed[:, lanes(i)] + jnp.dot(
+        total = acc_g[mixed(i)] + jnp.dot(
             q_ref[:, lanes(i)], prior.astype(bf), preferred_element_type=f32
         )
         mean_square = jnp.mean(total * total, axis=-1, keepdims=True)
@@ -465,9 +507,9 @@
             res[:, home(c, i)] = residual
             value = residual.astype(f32)
             square[...] += value * value
-            gath[h, :, seg(c, i)] = (value * model_ref[:, home(c, i)]).astype(bf)
+            gath[band(h), seg(c, i)] = (value * model_ref[:, home(c, i)]).astype(bf)
         for target in (near, other) if relayed else [line(d) for d in range(1, heads)]:
-            gather_send(gath.at[h, :, cols(c)], c, target).start()
+            gather_send(gath.at[band(h), cols(c)], c, target).start()
 
     def pass_on(c):
         if not relayed:
@@ -475,8 +517,8 @@
 
         @pl.when(inner)
         def _():
-            settled(gath.at[pl.ds(0, 3), :, cols(c)], gr.at[c])
-            gather_send(gath.at[pl.ds(2 - 2 * low, 2), :, cols(c)], c, near).start()
+            settled(gath.at[band(0, 3), cols(c)], gr.at[c])
+            gather_send(gath.at[band(2 - 2 * low, 2), cols(c)], c, near).start()
 
     def settle_norm():
         mean_square = jnp.sum(square[...], axis=1, keepdims=True) / width
@@ -484,45 +526,70 @@
         high = factor.astype(bf).astype(f32)
         rest = (factor - high).astype(bf).astype(f32)
         at = lax.broadcasted_iota(jnp.int32, (rows, 128), 1)
-        rgath[h] = jnp.where(at < 64, high, rest).astype(bf)
+        rgath[band(h), :] = jnp.where(at < 64, high, rest).astype(bf)
         for d in range(1, heads):
-            at = rgath.at[h]
+            at = rgath.at[band(h), :]
             remote(at, at, gs.at[1], gr.at[chunks], s, line(d)).start()
 
-    def own_copy(c):
-        return pltpu.make_async_copy(send.at[s, :, cols(c)], recv.at[s, :, cols(c)], pr.at[c])
+    def choose(c, work):
+        if not woven:
+            work(0)
+            return
+        for o in range(2):
+
+            @pl.when(c % 2 == o)
+            def _(o=o):
+                work(o)
+
+    def scatter(o, who, source, size, at, c, buffers):
+        out, target, psem, _ = buffers
+        picked = jnp.dot(pick_ref[o, who], source, preferred_element_type=f32)
+        here = pl.ds(who * count, count)
+        out[here, :, at] = picked.astype(bf).reshape(count, slots, size)
+        b1 = ways[o][0] if who else 0
+        order = range(count - 1, -1, -1)
+        for n in order:
+            d = lists[o][n]
+            src = out.at[who * count + n, :, at]
+            dst = target.at[d ^ b1, :, at]
+            if d == 0:
+                pltpu.make_async_copy(src, dst, pr.at[c]).start()
+            else:
+                remote(src, dst, psem, pr.at[c], flip(d), h).start()
+
+    def spread_rows(o, gathered, beside, at, size, c, buffers):
+        dsem = buffers[3]
+        if woven:
+            remote(
+                gathered.at[:, at], beside.at[:, at], dsem, nr.at[c], flip(ways[o][0]), h
+            ).start()
+        scatter(o, 0, gathered[:, at], size, at, c, buffers)
+
+    def relay_rows(o, beside, at, size, c, buffers):
+        settled(beside.at[:, at], nr.at[c])
+        scatter(o, 1, beside[:, at], size, at, c, buffers)
 
     def dispatch(c):
         def arrived():
-            settled(gath.at[pl.ds(0, heads - 1), :, cols(c)], gr.at[c])
+            settled(gath.at[band(0, heads - 1), cols(c)], gr.at[c])
 
         if relayed:
             pl.when(jnp.logical_not(inner))(arrived)
         else:
             arrived()
-        picked = jnp.dot(
-            pick_ref[...], gath[:, :, cols(c)].reshape(tokens, step),
-            preferred_element_type=f32,
-        )
-        send[:, :, cols(c)] = picked.astype(bf).reshape(seqs, slots, step)
-        for d in far:
-            remote(
-                send.at[flip(d), :, cols(c)], recv.at[s, :, cols(c)], ps.at[0], pr.at[c],
-                flip(d), h,
-            ).start()
-        own_copy(c).start()
+        choose(c, lambda o: spread_rows(o, gath, nbr, cols(c), step, c, (send, recv, ps.at[0], ds.at[0])))
+
+    def relay(c):
+        if woven:
+            choose(c, lambda o: relay_rows(o, nbr, cols(c), step, c, (send, recv, ps.at[0], ds.at[0])))
 
     def dispatch_norm():
-        settled(rgath.at[pl.ds(0, heads - 1)], gr.at[chunks])
-        picked = jnp.dot(
-            pick_ref[...], rgath[...].reshape(tokens, 128), preferred_element_type=f32
-        )
-        rsend[...] = picked.astype(bf).reshape(seqs, slots, 128)
-        for d in far:
-            remote(
-                rsend.at[flip(d)], rrecv.at[s], ps.at[1], pr.at[chunks], flip(d), h
-            ).start()
-        pltpu.make_async_copy(rsend.at[s], rrecv.at[s], pr.at[chunks]).start()
+        settled(rgath.at[band(0, heads - 1), :], gr.at[chunks])
+        spread_rows(0, rgath, rnbr, pl.ds(0, 128), 128, chunks, (rsend, rrecv, ps.at[1], ds.at[1]))
+
+    def relay_norm():
+        if woven:
+            relay_rows(0, rnbr, pl.ds(0, 128), 128, chunks, (rsend, rrecv, ps.at[1], ds.at[1]))
 
     def expand(c):
         pltpu.make_async_copy(
@@ -543,13 +610,17 @@
 
     w_far(0)
     w_passed(0)
-    depth = 6
+    depth = 7 if woven else 6
 
     def stage(t, lag, work):
         @pl.when((t >= lag) & (t < chunks + lag))
         def _():
             work(t - lag)
 
+    def release(j, carry):
+        w_drain(j)
+        return carry
+
     def forward(t, carry):
         j = (t + 2) // 2
 
@@ -567,6 +638,7 @@
             w_passed(j)
 
         stage(t, 4, dispatch)
+        stage(t, 5, relay)
         stage(t, 3, pass_on)
         stage(t, 2, settle)
 
@@ -577,24 +649,31 @@
         stage(t, 1, merge)
         stage(t, 0, project)
 
+        @pl.when(t == 0)
+        def _():
+            routing()
+
+        @pl.when(t == chunks + 2)
+        def _():
+            lax.fori_loop(0, subs, release, 0)
+
         @pl.when(t == chunks + 3)
         def _():
             dispatch_norm()
 
+        @pl.when(t == chunks + 4)
+        def _():
+            relay_norm()
+
         stage(t, depth, expand)
         return carry
 
     lax.fori_loop(0, chunks + depth, forward, 0)
-
-    def release(j, carry):
-        w_drain(j)
-        return carry
 
     def start_down(c, carry):
         down_copy(c).start()
         return carry
 
-    lax.fori_loop(0, subs, release, 0)
     lax.fori_loop(0, chunks, start_down, 0)
     settled(psend.at[pl.ds(0, heads - 1)], zs)
     settled(rrecv, pr.at[chunks])
@@ -612,7 +691,7 @@
 
     lax.fori_loop(0, seqs, activate, 0)
 
-    def contract(c, carry):
+    def contract(c):
         @pl.when(c % 2 == 0)
         def _():
             down_copy(c // 2).wait()
@@ -624,23 +703,61 @@
             preferred_element_type=f32,
         )
         recv[:, :, at] = (rows_out * down_scale).astype(bf).reshape(seqs, slots, fine)
-        for d in far:
+
+        def give(o):
+            for who in (1, 0) if woven else (0,):
+                b1 = ways[o][0] if who else 0
+                sem = (rl if who else rr).at[c]
+                for n in range(count - 1, -1, -1):
+                    d = lists[o][n]
+                    src = recv.at[d ^ b1, :, at]
+                    dst = back.at[who * count + n, :, at]
+                    if d == 0:
+                        pltpu.make_async_copy(src, dst, sem).start()
+                    else:
+                        remote(src, dst, rs, sem, flip(d), h).start()
+
+        choose(c, give)
+
+    def landing(c):
+        return wbuf.at[
+            c // 2,
+            pl.ds(hidden, tokens),
+            pl.ds(pl.multiple_of((c % 2) * fine, fine), fine),
+        ]
+
+    def unite(c):
+        at = fcols(c)
+        settled(back.at[pl.ds(count, count), :, at], rl.at[c])
+
+        def work(o):
+            total = jnp.dot(
+                mix_ref[o, 1], back[pl.ds(count, count), :, at].reshape(owned, fine),
+                preferred_element_type=f32,
+            )
+            nbr[:, at] = total.astype(bf)
             remote(
-                recv.at[flip(d), :, at], back.at[s, :, at], rs, rr.at[c], flip(d), h
+                nbr.at[:, at], landing(c), es, er.at[c], flip(ways[o][0]), h
             ).start()
-        pltpu.make_async_copy(recv.at[s, :, at], back.at[s, :, at], rr.at[c]).start()
-        return carry
-
-    lax.fori_loop(0, pieces, contract, 0)
+
+        choose(c, work)
 
     def combine(c):
         at = fcols(c)
-        settled(back.at[:, :, at], rr.at[c])
-        total = jnp.dot(
-            mix_ref[...], back[:, :, at].reshape(seqs * slots, fine),
-            preferred_element_type=f32,
-        )
-        split_heads(total, at, fine)
+        settled(back.at[pl.ds(0, count), :, at], rr.at[c])
+        if woven:
+            settled(landing(c), er.at[c])
+
+        def work(o):
+            total = jnp.dot(
+                mix_ref[o, 0], back[pl.ds(0, count), :, at].reshape(owned, fine),
+                preferred_element_type=f32,
+            )
+            if woven:
+                total = total + landing(c)[...].astype(f32)
+            split_heads(total, at, fine)
+
+        choose(c, work)
         for d in range(1, heads):
             remote(
                 psend.at[line(d), :, at], precv.at[h, :, at], cs, cr.at[c], s, line(d)
@@ -654,18 +771,20 @@
             total = total + precv[line(d), :, at].astype(f32)
         out_ref[:, at] = total.astype(bf)
 
+    lags = (0, 2, 4, 6) if woven else (0, 0, 3, 5)
+
     def backward(t, carry):
-        @pl.when(t < pieces)
-        def _():
-            combine(t)
-
-        @pl.when(t >= 2)
-        def _():
-            finish(t - 2)
-
-        return carry
-
-    lax.fori_loop(0, pieces + 2, backward, 0)
+        for lag, work in zip(lags, (contract, unite, combine, finish)):
+            if work is unite and not woven:
+                continue
+
+            @pl.when((t >= lag) & (t < pieces + lag))
+            def _(lag=lag, work=work):
+                work(t - lag)
+
+        return carry
+
+    lax.fori_loop(0, pieces + lags[-1], backward, 0)
 
     state_swap().wait_send()
     settled(pair_state.at[pl.ds(0, owners - 1), pl.ds(0, local // 2)], pair_s)
@@ -679,14 +798,20 @@
 
         @pl.when(jnp.logical_not(inner))
         def _():
-            settled(gath.at[pl.ds(0, 2)], gs.at[0])
+            settled(gath.at[band(0, 2), :], gs.at[0])
     else:
-        settled(gath.at[pl.ds(0, heads - 1)], gs.at[0])
-    settled(rgath.at[pl.ds(0, heads - 1)], gs.at[1])
-    settled(send.at[pl.ds(0, seqs - 1)], ps.at[0])
-    settled(rsend.at[pl.ds(0, seqs - 1)], ps.at[1])
-    settled(recv.at[pl.ds(0, seqs - 1)], rs)
+        settled(gath.at[band(0, heads - 1), :], gs.at[0])
+    settled(rgath.at[band(0, heads - 1), :], gs.at[1])
+    moved = seqs - 2 if woven else seqs - 1
+    settled(send.at[pl.ds(0, moved)], ps.at[0])
+    settled(rsend.at[pl.ds(0, moved)], ps.at[1])
+    settled(recv.at[pl.ds(0, moved)], rs)
     settled(psend.at[pl.ds(0, heads - 1)], cs)
+    if woven:
+        settled(near_route, near_s)
+        settled(nbr, ds.at[0])
+        settled(rnbr, ds.at[1])
+        settled(nbr, es)
 
 
 def body(
@@ -714,8 +839,12 @@
     owners = seqs // 2
     chunks = 2 * subs
     step = owners * SEG
+    woven = seqs == 8
+    ways, sides = (2, 2) if woven else (1, 1)
     capacity = 3 * rows * TOPK // (2 * seqs * heads)
     slots = -(-capacity * heads // 16) * 16
+    owned = (4 if woven else seqs) * slots
+    deep = max(features, hidden + tokens if woven else hidden)
     vmem = pl.BlockSpec(memory_space=pltpu.VMEM)
     smem = pl.BlockSpec(memory_space=pltpu.SMEM)
     anywhere = pl.BlockSpec(memory_space=pl.ANY)
@@ -733,9 +862,8 @@
             pltpu.VMEM((rows, width), bf),
             pltpu.VMEM((2, local, HD, HD), bf),
             pltpu.VMEM((owners, local, HD, HD), bf),
-            pltpu.VMEM((tokens, features), f32),
             pltpu.VMEM((tokens, features), bf),
-            pltpu.VMEM((chunks, max(features, hidden), step), bf),
+            pltpu.VMEM((chunks, deep, step), bf),
             pltpu.VMEM((heads, rows, step), f32),
             pltpu.VMEM((rows, width), f32),
             pltpu.VMEM((heads, rows, width), bf),
@@ -743,16 +871,20 @@
             pltpu.VMEM((rows, width), bf),
             pltpu.VMEM((rows, SEG), f32),
             pltpu.VMEM((128, 128), f32),
-            pltpu.VMEM((heads, 2, rows, 128), f32),
-            pltpu.VMEM((seqs * slots, tokens), bf),
-            pltpu.VMEM((tokens, seqs * slots), bf),
+            pltpu.VMEM((heads, 2 * TOPK, 128), f32),
+            pltpu.VMEM((2, heads, 2 * TOPK, 128), f32),
+            pltpu.VMEM((heads, rows, 128), f32),
+            pltpu.VMEM((ways, sides, owned, tokens), bf),
+            pltpu.VMEM((ways, sides, tokens, owned), bf),
             pltpu.VMEM((width, hidden), bf),
             pltpu.VMEM((width, hidden), bf),
-            pltpu.VMEM((heads, rows, width), bf),
+            pltpu.VMEM((tokens, width), bf),
+            pltpu.VMEM((tokens, width if woven else 128), bf),
             pltpu.VMEM((seqs, slots, width), bf),
             pltpu.VMEM((seqs, slots, width), bf),
             pltpu.VMEM((seqs, slots, width), bf),
-            pltpu.VMEM((heads, rows, 128), bf),
+            pltpu.VMEM((tokens, 128), bf),
+            pltpu.VMEM((tokens, 128), bf),
             pltpu.VMEM((seqs, slots, 128), bf),
             pltpu.VMEM((seqs, slots, 128), bf),
             pltpu.VMEM((seqs * slots, hidden), f32),
@@ -768,12 +900,19 @@
             dma((subs,)),
             dma((2,)),
             dma,
+            dma((2,)),
+            dma,
             dma((chunks,)),
             dma((chunks,)),
             dma((2,)),
             dma((chunks + 1,)),
             dma((2,)),
             dma((chunks + 1,)),
+            dma((2,)),
+            dma((chunks + 1,)),
+            dma,
+            dma((2 * chunks,)),
+            dma((2 * chunks,)),
             dma,
             dma((2 * chunks,)),
             dma,

time: 205 us -> 189 us (0.922)
  Pallas kernels: 203 us -> 187 us
    pallas_call x1, Pallas kernels: 203 us -> 187 us  [body(): pl.pallas_call(functools.partial(layer_kernel, seqs, heads, slots), out_s...]
where the time goes in v2:
time: 189 us; the launch traced here: 188 us
  Pallas kernels  187 us (99%)
    pallas_call x1, Pallas kernels, body(): pl.pallas_call(functools.partial(layer_kernel, seqs, heads, slots), out_s...  187 us

profile of v2, /device:TPU:0, one launch (start us, length us, event | category | flops | bytes accessed | tf_op | source)
XLA Modules:
  0.0 188.4 jit_solution(11165153450412651357)
XLA Ops:
  0.0 186.5 %shard_map.127 = bf16[64,4096]{1,0:T(8,128)(2,1)} custom-call(bf16[256,1024]{1,0:T(8,128)(2,1)} %q_hbm.1, bf16[256,1024]{1,0:T(8,128)(2,1)} %k_hbm.1, bf16[256,1024]{1,0:T(8,128)(2,1)} %v_hbm.1, f32[1,1024]{1,0:T(1,128)} %bitcast.5, bf16[1024,512]{1,0:T(8,128)(2,1)} %w_hbm.1, bf16[64,4096]{1,0:T(8,128)(2,1)} %stream_hbm.1, f32[1,4096]{1,0:T(1,128)} %bitcast.4, ...), custom_call_target="tpu_custom_call" | custom-call | tf_op jit(solution)/shard_map/pallas_call | solution.py:853
  186.5 1.9 copy.15
